TPU v7x, 32 devices: a whole 2x2x4 slice. The times are simulated.
32 devices in a mesh: grp: 2 (over core), dp: 4 (over y, x), sp: 4 (over z).
Axes of the slice: x: 2, y: 2, z: 4, core: 2. Of those that a mesh axis runs over, the one named last changes fastest.
Arguments:
- vis: bfloat16 [512, 5120], P(('grp', 'dp', 'sp')), may hold values from -6 to 6
- merge_weight: bfloat16 [5120, 8192], P('dp', ('grp', 'sp')), may hold values from -0.078125 to 0.078125
- img_counts: int32 [32], P('dp'), may hold values from 1 to 16
- img_pos: int32 [512], P(('grp', 'dp', 'sp')), may hold values from 0 to 127, as said below
- text: bfloat16 [4096, 8192], P(('grp', 'dp', 'sp')), may hold values from -6 to 6
- cot: bfloat16 [4096, 8192], P(('grp', 'dp', 'sp')), may hold values from -6 to 6
- gain: float32 [8192], replicated, may hold values from 0.25 to 1.75
Outputs:
- vis_grad: bfloat16 [512, 5120], P(('grp', 'dp', 'sp'))
- gain_grad: float32 [8192], replicated
Inputs may be any that keep to these rules, and one draw needn't show every extreme that they name: `img_pos`: within one device's block the 16 positions are distinct. `img_counts`: the counts of one image group sum to at most 128.
All inputs are finite; a program needn't handle non-finite values.
Results may differ from a plain program's by a relative error of at most 0.014.
Values may be sent and summed in bfloat16 or wider, within the bound.
No kernel may reach another device: no remote copies, remote signals or barrier semaphores. Data moves between devices by JAX's collectives and lax.ppermute only.
A program may use at most 128 MiB of HBM per device.

v0:
```python
import jax
import jax.numpy as jnp
from jax import lax
from jax.sharding import PartitionSpec as P


def body(vis, merge_weight, img_counts, img_pos, text, cot, gain):
    rows_dev = vis.shape[0]
    tok_rows = text.shape[0]
    group_vis = lax.all_gather(vis, ("grp", "sp"), axis=0, tiled=True)
    full_weight = lax.all_gather(merge_weight, "dp", axis=0, tiled=True)
    partial_value = jnp.dot(group_vis, full_weight, preferred_element_type=jnp.float32)
    emb = lax.all_to_all(
        partial_value.astype(jnp.bfloat16), ("grp", "sp"), split_axis=0, concat_axis=1, tiled=True
    )
    total_live = jnp.sum(img_counts)
    member = lax.axis_index("grp") * lax.axis_size("sp") + lax.axis_index("sp")
    group_row = member * rows_dev + jnp.arange(rows_dev, dtype=jnp.int32)
    live = group_row < total_live
    places = jnp.arange(tok_rows, dtype=jnp.int32)
    select = (img_pos[None, :] == places[:, None]) & live[None, :]
    taken = jnp.any(select, axis=1)
    select_b = select.astype(jnp.bfloat16)
    placed = jnp.dot(select_b, emb, preferred_element_type=jnp.float32)
    hidden = jnp.where(taken[:, None], placed, text.astype(jnp.float32))
    rinv = lax.rsqrt(jnp.mean(hidden * hidden, axis=1, keepdims=True) + 1e-06)
    cotf = cot.astype(jnp.float32)
    part_gain = jnp.sum(cotf * hidden * rinv, axis=0)
    scaled = cotf * gain[None, :]
    inner = jnp.mean(scaled * hidden, axis=1, keepdims=True)
    dhid = (rinv * scaled - hidden * rinv**3 * inner).astype(jnp.bfloat16)
    demb = jnp.dot(select_b.T, dhid, preferred_element_type=jnp.float32)
    demb = jnp.where(live[:, None], demb, 0.0).astype(jnp.bfloat16)
    returned = lax.all_to_all(demb, ("grp", "sp"), split_axis=1, concat_axis=0, tiled=True)
    terms = lax.dot_general(
        returned, full_weight, (((1,), (1,)), ((), ())), preferred_element_type=jnp.float32
    )
    vis_grad = lax.psum_scatter(
        terms.astype(jnp.bfloat16), ("grp", "sp"), scatter_dimension=0, tiled=True
    )
    gain_grad = lax.psum(part_gain, ("grp", "dp", "sp"))
    return (vis_grad, gain_grad)


def solution(mesh):
    return jax.shard_map(
        body,
        mesh=mesh,
        in_specs=(
            P(("grp", "dp", "sp"), None),
            P("dp", ("grp", "sp")),
            P("dp"),
            P(("grp", "dp", "sp")),
            P(("grp", "dp", "sp"), None),
            P(("grp", "dp", "sp"), None),
            P(),
        ),
        out_specs=(P(("grp", "dp", "sp"), None), P()),
        check_vma=False,
    )
```

profile of v0, /device:TPU:0, one launch (start us, length us, event | category | flops | bytes accessed | tf_op | source)
XLA Modules:
  0.0 229.6 jit_solution(17347707635758896386)
XLA Ops:
  7.2 0.0 all-gather.3.cloned.1.call-start
  7.2 0.7 all-gather.3.cloned.1.call-update
  7.9 0.0 all-gather.5.cloned.1.call-start
  7.9 0.7 all-gather.5.cloned.1.call-update
  8.6 0.0 copy-start.4
  8.7 0.0 copy-start.3
  8.7 0.0 copy-start
  8.7 27.1 %all-gather.3.cloned.1.call-done = bf16[128,5120]{1,0:T(8,128)(2,1)} async-done(((bf16[16,5120]{1,0:T(8,128)(2,1)}), bf16[128,5120]{1,0:T(8,128)(2,1)}) %all-gather.3.cloned.1.call-update) | async-done | bytes 1310736 | tf_op jit(solution)/shard_map/all_gather | solution.py:10
  35.7 106.3 %all-gather.5.cloned.1.call-done = bf16[5120,1024]{1,0:T(8,128)(2,1)} async-done(((bf16[1280,1024]{1,0:T(8,128)(2,1)}), bf16[5120,1024]{1,0:T(8,128)(2,1)}) %all-gather.5.cloned.1.call-update) | async-done | bytes 10485776 | tf_op jit(solution)/shard_map/all_gather | solution.py:11
  142.1 6.6 %convolution_convert_fusion.1 = bf16[128,1024]{1,0:T(8,128)(2,1)} fusion(bf16[128,5120]{1,0:T(8,128)(2,1)} %all-gather.3.cloned.1.call-done, bf16[5120,1024]{1,0:T(8,128)(2,1)} %all-gather.5.cloned.1.call-done), kind=kOutput, calls=%fused_computation.14 | convolution fusion | flops 1342308352 | bytes 12058624 | tf_op jit(solution)/shard_map/dot_general | solution.py:12
  148.7 0.0 copy-start.2
  148.7 4.7 %all-to-all-start = ((bf16[8,16,1024]{2,1,0:T(8,128)(2,1)}), bf16[8,16,1024]{2,1,0:T(8,128)(2,1)S(1)}, u32[]{:S(2)}, u32[]{:S(2)}) async-start(bf16[8,16,1024]{2,1,0:T(8,128)(2,1)} %bitcast), calls=%async_computation | async-start | bytes 524288 | tf_op jit(solution)/shard_map/all_to_all | solution.py:13
  153.4 0.0 reduce-scatter.2.cloned.1.call-start
  153.5 0.0 copy-done.4
  153.5 0.6 reduce_sum.36
  154.1 0.7 add_compare_fusion
  154.8 0.0 copy-done.3
  154.8 0.1 fusion.12
  154.9 7.9 %all-to-all-done = bf16[8,16,1024]{2,1,0:T(8,128)(2,1)S(1)} async-done(((bf16[8,16,1024]{2,1,0:T(8,128)(2,1)}), bf16[8,16,1024]{2,1,0:T(8,128)(2,1)S(1)}, u32[]{:S(2)}, u32[]{:S(2)}) %all-to-all-start) | async-done | bytes 262176 | tf_op jit(solution)/shard_map/all_to_all | solution.py:13
  162.8 0.0 copy-start.1
  162.8 0.0 copy-done
  162.8 0.0 slice-start
  162.8 1.0 multiply_reduce_fusion
  163.8 0.0 copy-done.2
  163.8 0.6 copy-done.1
  164.4 0.0 slice-start.1
  164.4 1.5 fusion.7
  165.9 0.0 slice-start.2
  165.9 1.1 fusion
  167.1 11.8 %all_to_all.38 = bf16[16,8,1024]{2,0,1:T(8,128)(2,1)S(1)} all-to-all(bf16[16,8,1024]{2,0,1:T(8,128)(2,1)S(1)} %bitcast.21), channel_id=1, replica_groups=mesh['grp'=2,'dp'=4,'sp'=4] {'grp','sp'}, dimensions={1} | all-to-all | bytes 524288 | tf_op jit(solution)/shard_map/all_to_all | solution.py:34
  178.8 0.0 slice-done
  178.9 0.0 slice-done.1
  178.9 0.0 slice-done.2
  178.9 4.6 %convolution_convert_fusion = bf16[128,5120]{1,0:T(8,128)(2,1)} fusion(bf16[128,1024]{1,0:T(8,128)(2,1)S(1)} %bitcast.19, bf16[5120,1024]{1,0:T(8,128)(2,1)S(1)} %bitcast.17), kind=kOutput, calls=%fused_computation.3 | convolution fusion | flops 1342832640 | bytes 12058624 | tf_op jit(solution)/shard_map/dot_general | solution.py:35
  183.5 0.0 reduce-scatter.2.cloned.1.call-update
  183.5 39.5 %psum.7 = f32[8192]{0:T(1024)} all-reduce(f32[8192]{0:T(1024)S(1)} %get-tuple-element.2), channel_id=1, replica_groups=mesh['grp'=2,'dp'=4,'sp'=4] {'grp','dp','sp'}, use_global_device_ids=true, to_apply=%region_6.7 | all-reduce | flops 8192 | bytes 65536 | tf_op jit(solution)/shard_map/psum | solution.py:41
  223.0 0.0 reduce-scatter.2.cloned.1.call-done
  (5 shorter events, 0.1 us)
Async XLA Ops:
  7.2 28.6 %all-gather.3.cloned.1.call-start = ((), (), s32[]{:S(2)}) async-start(), calls=%async_computation.3 | async-start | bytes 1474560 | tf_op jit(solution)/shard_map/all_gather | solution.py:10
  7.9 134.2 %all-gather.5.cloned.1.call-start = ((), (), s32[]{:S(2)}) async-start(), calls=%async_computation.4 | async-start | bytes 13107200 | tf_op jit(solution)/shard_map/all_gather | solution.py:11
  8.6 144.8 %copy-start.4 = (s32[8]{0:T(128)S(1)}, s32[8]{0:T(128)}, u32[]{:S(2)}) copy-start(s32[8]{0:T(128)} %param.9) | copy-start | bytes 100
  8.7 146.1 %copy-start.3 = (s32[16]{0:T(128)S(1)}, s32[16]{0:T(128)}, u32[]{:S(2)}) copy-start(s32[16]{0:T(128)} %param.10) | copy-start | bytes 196
  8.7 154.1 %copy-start = (bf16[128,8192]{1,0:T(8,128)(2,1)S(1)}, bf16[128,8192]{1,0:T(8,128)(2,1)}, u32[]{:S(2)}) copy-start(bf16[128,8192]{1,0:T(8,128)(2,1)} %param.11) | copy-start | bytes 6291460
  148.7 15.1 %copy-start.2 = (f32[8192]{0:T(1024)S(1)}, f32[8192]{0:T(1024)}, u32[]{:S(2)}) copy-start(f32[8192]{0:T(1024)} %param.13) | copy-start | bytes 98308
  148.7 14.1 %all-to-all-start = ((bf16[8,16,1024]{2,1,0:T(8,128)(2,1)}), bf16[8,16,1024]{2,1,0:T(8,128)(2,1)S(1)}, u32[]{:S(2)}, u32[]{:S(2)}) async-start(bf16[8,16,1024]{2,1,0:T(8,128)(2,1)} %bitcast), calls=%async_computation | async-start | bytes 524288 | tf_op jit(solution)/shard_map/all_to_all | solution.py:13
  153.4 69.6 %reduce-scatter.2.cloned.1.call-start = ((), (), s32[]{:S(2)}) async-start(), calls=%async_computation.5 | async-start | bytes 1474560 | tf_op jit(solution)/shard_map/reduce_scatter | solution.py:38
  162.8 1.6 copy-start.1
  162.8 16.0 %slice-start = ((s8[10485760]{0:T(1024)(128)(4,1)}), s8[4194304]{0:T(1024)(128)(4,1)S(1)}, s32[]{:S(2)}) async-start(s8[10485760]{0:T(1024)(128)(4,1)} %bitcast.16), calls=%async_computation.6 | async-start | bytes 8388608
  164.4 14.5 %slice-start.1 = ((s8[10485760]{0:T(1024)(128)(4,1)}), s8[4194304]{0:T(1024)(128)(4,1)S(1)}, s32[]{:S(2)}) async-start(s8[10485760]{0:T(1024)(128)(4,1)} %bitcast.16), calls=%async_computation.7 | async-start | bytes 8388608
  165.9 13.0 %slice-start.2 = ((s8[10485760]{0:T(1024)(128)(4,1)}), s8[2097152]{0:T(1024)(128)(4,1)S(1)}, s32[]{:S(2)}) async-start(s8[10485760]{0:T(1024)(128)(4,1)} %bitcast.16), calls=%async_computation.8 | async-start | bytes 4194304
Sparse Core Ops, SparseCore 0:
  9.6 26.1 all-gather.2
  37.6 104.4 all-gather.4
  183.6 34.8 reduce-scatter.1
where the time goes:
time: 230 us
  waiting for transfers between devices  143 us (62%)
  blocking collectives  51.3 us (22%)
  between operations  13.9 us (6%)
  matrix products  13.4 us (6%)
  starting transfers between devices  4.85 us (2%)
  other arithmetic  2.91 us (1%)
    all_gather x1, waiting for transfers between devices, body(): full_weight = lax.all_gather(merge_weight, 'dp', axis=0, tiled=True)  106 us
    psum x1, blocking collectives, body(): gain_grad = lax.psum(part_gain, ('grp', 'dp', 'sp'))  39.5 us
    all_gather x1, waiting for transfers between devices, body(): group_vis = lax.all_gather(vis, ('grp', 'sp'), axis=0, tiled=True)  27.1 us
    all_to_all x1, blocking collectives, body(): lax.all_to_all(demb, ('grp', 'sp'), split_axis=1, concat_axis=0, tiled=True)  11.8 us
    all_to_all x1, waiting for transfers between devices, body(): lax.all_to_all(partial_value.astype(jnp.bfloat16), ('grp', 'sp'), split_a...  7.9 us
    dot_general x1, matrix products, body(): jnp.dot(group_vis, full_weight, preferred_element_type=jnp.float32)  6.62 us
    all_to_all x1, starting transfers between devices, body(): lax.all_to_all(partial_value.astype(jnp.bfloat16), ('grp', 'sp'), split_a...  4.74 us
    dot_general x1, matrix products, body(): lax.dot_general(returned, full_weight, (((1,), (1,)), ((), ())), preferre...  4.62 us
  transfers between devices with their start and end apart: 4, of which 3 were waited for; matrix products, arithmetic and copies ran while one was open for 1% of the time, Pallas kernels for 0%

commit v1 on v0

--- a/solution.py
+++ b/solution.py
@@ -10,8 +10,16 @@
     group_vis = lax.all_gather(vis, ("grp", "sp"), axis=0, tiled=True)
     full_weight = lax.all_gather(merge_weight, "dp", axis=0, tiled=True)
     partial_value = jnp.dot(group_vis, full_weight, preferred_element_type=jnp.float32)
-    emb = lax.all_to_all(
-        partial_value.astype(jnp.bfloat16), ("grp", "sp"), split_axis=0, concat_axis=1, tiled=True
+    emb = jnp.concatenate(
+        lax.all_to_all(
+            jnp.stack(
+                jnp.split(partial_value.astype(jnp.bfloat16), lax.axis_size(("grp", "sp")), axis=0)
+            ),
+            ("grp", "sp"),
+            0,
+            0,
+        ),
+        axis=1,
     )
     total_live = jnp.sum(img_counts)
     member = lax.axis_index("grp") * lax.axis_size("sp") + lax.axis_index("sp")

time: 230 us -> 234 us (1.017)
  local copies, waits for them, and re-layouts: 0.62 us -> 5.52 us
    unnamed x16 -> x23, local copies, waits for them, and re-layouts: 0.59 us -> 4.88 us
where the time goes in v1:
time: 234 us
  waiting for transfers between devices  143 us (61%)
  blocking collectives  51.3 us (22%)
  between operations  13.9 us (6%)
  matrix products  12.7 us (5%)
  local copies, waits for them, and re-layouts  5.52 us (2%)
  starting transfers between devices  4.72 us (2%)
  other arithmetic  2.91 us (1%)
    all_gather x1, waiting for transfers between devices, body(): full_weight = lax.all_gather(merge_weight, 'dp', axis=0, tiled=True)  106 us
    psum x1, blocking collectives, body(): gain_grad = lax.psum(part_gain, ('grp', 'dp', 'sp'))  39.5 us
    all_gather x1, waiting for transfers between devices, body(): group_vis = lax.all_gather(vis, ('grp', 'sp'), axis=0, tiled=True)  27.1 us
    all_to_all x1, blocking collectives, body(): lax.all_to_all(demb, ('grp', 'sp'), split_axis=1, concat_axis=0, tiled=True)  11.8 us
    all_to_all x1, waiting for transfers between devices, body(): lax.all_to_all(jnp.stack(jnp.split(partial_value.astype(jnp.bfloat16), la...  7.9 us
    dot_general x1, matrix products, body(): jnp.dot(group_vis, full_weight, preferred_element_type=jnp.float32)  5.91 us
    unnamed x23, local copies, waits for them, and re-layouts  4.88 us
  transfers between devices with their start and end apart: 4, of which 3 were waited for; matrix products, arithmetic and copies ran while one was open for 1% of the time, Pallas kernels for 0%

profile of v1, /device:TPU:0, one launch (start us, length us, event | category | flops | bytes accessed | tf_op | source)
XLA Modules:
  0.0 233.6 jit_solution(17112159985192227094)
XLA Ops:
  7.2 0.0 all-gather.3.cloned.1.call-start
  7.2 0.7 all-gather.3.cloned.1.call-update
  7.9 0.0 all-gather.5.cloned.1.call-start
  7.9 0.7 all-gather.5.cloned.1.call-update
  8.6 0.0 copy-start.4
  8.7 0.0 copy-start.3
  8.7 0.0 copy-start
  8.7 27.1 %all-gather.3.cloned.1.call-done = bf16[128,5120]{1,0:T(8,128)(2,1)} async-done(((bf16[16,5120]{1,0:T(8,128)(2,1)}), bf16[128,5120]{1,0:T(8,128)(2,1)}) %all-gather.3.cloned.1.call-update) | async-done | bytes 1310736 | tf_op jit(solution)/shard_map/all_gather | solution.py:10
  35.7 106.3 %all-gather.5.cloned.1.call-done = bf16[5120,1024]{1,0:T(8,128)(2,1)} async-done(((bf16[1280,1024]{1,0:T(8,128)(2,1)}), bf16[5120,1024]{1,0:T(8,128)(2,1)}) %all-gather.5.cloned.1.call-update) | async-done | bytes 10485776 | tf_op jit(solution)/shard_map/all_gather | solution.py:11
  142.1 5.9 %convolution_convert_fusion.1 = bf16[128,1024]{1,0:T(8,128)(2,1)S(1)} fusion(bf16[128,5120]{1,0:T(8,128)(2,1)} %all-gather.3.cloned.1.call-done, bf16[5120,1024]{1,0:T(8,128)(2,1)} %all-gather.5.cloned.1.call-done), kind=kOutput, calls=%fused_computation.14 | convolution fusion | flops 1342308352 | bytes 12058624 | tf_op jit(solution)/shard_map/dot_general | solution.py:12
  148.0 0.0 copy-start.2
  148.0 0.6 fusion.16
  148.6 0.6 fusion.15
  149.2 0.6 fusion.14
  149.8 0.6 fusion.13
  150.5 0.6 fusion.12
  151.1 0.6 fusion.11
  151.7 0.6 fusion.10
  152.3 0.6 fusion.9
  152.9 4.6 %all-to-all-start = ((bf16[8,16,1024]{2,1,0:T(8,128)(2,1)}), bf16[8,16,1024]{2,1,0:T(8,128)(2,1)S(1)}, u32[]{:S(2)}, u32[]{:S(2)}) async-start(bf16[8,16,1024]{2,1,0:T(8,128)(2,1)} %fusion.9), calls=%async_computation | async-start | bytes 524288 | tf_op jit(solution)/shard_map/all_to_all | solution.py:14
  157.5 0.0 reduce-scatter.2.cloned.1.call-start
  157.6 0.0 copy-done.4
  157.6 0.6 reduce_sum.36
  158.2 0.7 add_compare_fusion
  158.9 0.0 copy-done.3
  158.9 0.1 fusion.20
  159.0 7.9 %all-to-all-done = bf16[8,16,1024]{2,1,0:T(8,128)(2,1)S(1)} async-done(((bf16[8,16,1024]{2,1,0:T(8,128)(2,1)}), bf16[8,16,1024]{2,1,0:T(8,128)(2,1)S(1)}, u32[]{:S(2)}, u32[]{:S(2)}) %all-to-all-start) | async-done | bytes 262176 | tf_op jit(solution)/shard_map/all_to_all | solution.py:14
  166.9 0.0 copy-start.1
  166.9 0.0 copy-done
  166.9 0.0 slice-start
  166.9 1.0 multiply_reduce_fusion
  167.9 0.0 copy-done.2
  167.9 0.6 copy-done.1
  168.5 0.0 slice-start.1
  168.5 1.5 fusion.7
  170.0 0.0 slice-start.2
  170.0 1.1 fusion
  171.2 11.8 %all_to_all.24 = bf16[16,8,1024]{2,0,1:T(8,128)(2,1)S(1)} all-to-all(bf16[16,8,1024]{2,0,1:T(8,128)(2,1)S(1)} %bitcast.52), channel_id=1, replica_groups=mesh['grp'=2,'dp'=4,'sp'=4] {'grp','sp'}, dimensions={1} | all-to-all | bytes 524288 | tf_op jit(solution)/shard_map/all_to_all | solution.py:42
  182.9 0.0 slice-done
  182.9 0.0 slice-done.1
  182.9 0.0 slice-done.2
  183.0 4.6 %convolution_convert_fusion = bf16[128,5120]{1,0:T(8,128)(2,1)} fusion(bf16[128,1024]{1,0:T(8,128)(2,1)S(1)} %bitcast.50, bf16[5120,1024]{1,0:T(8,128)(2,1)S(1)} %bitcast.48), kind=kOutput, calls=%fused_computation.3 | convolution fusion | flops 1342832640 | bytes 12058624 | tf_op jit(solution)/shard_map/dot_general | solution.py:43
  187.6 0.0 reduce-scatter.2.cloned.1.call-update
  187.6 39.5 %psum.7 = f32[8192]{0:T(1024)} all-reduce(f32[8192]{0:T(1024)S(1)} %get-tuple-element.2), channel_id=1, replica_groups=mesh['grp'=2,'dp'=4,'sp'=4] {'grp','dp','sp'}, use_global_device_ids=true, to_apply=%region_6.7 | all-reduce | flops 8192 | bytes 65536 | tf_op jit(solution)/shard_map/psum | solution.py:49
  227.1 0.0 reduce-scatter.2.cloned.1.call-done
  (5 shorter events, 0.1 us)
Async XLA Ops:
  7.2 28.6 %all-gather.3.cloned.1.call-start = ((), (), s32[]{:S(2)}) async-start(), calls=%async_computation.3 | async-start | bytes 1474560 | tf_op jit(solution)/shard_map/all_gather | solution.py:10
  7.9 134.2 %all-gather.5.cloned.1.call-start = ((), (), s32[]{:S(2)}) async-start(), calls=%async_computation.4 | async-start | bytes 13107200 | tf_op jit(solution)/shard_map/all_gather | solution.py:11
  8.6 148.9 %copy-start.4 = (s32[8]{0:T(128)S(1)}, s32[8]{0:T(128)}, u32[]{:S(2)}) copy-start(s32[8]{0:T(128)} %param.9) | copy-start | bytes 100
  8.7 150.2 %copy-start.3 = (s32[16]{0:T(128)S(1)}, s32[16]{0:T(128)}, u32[]{:S(2)}) copy-start(s32[16]{0:T(128)} %param.10) | copy-start | bytes 196
  8.7 158.2 %copy-start = (bf16[128,8192]{1,0:T(8,128)(2,1)S(1)}, bf16[128,8192]{1,0:T(8,128)(2,1)}, u32[]{:S(2)}) copy-start(bf16[128,8192]{1,0:T(8,128)(2,1)} %param.11) | copy-start | bytes 6291460
  148.0 19.9 %copy-start.2 = (f32[8192]{0:T(1024)S(1)}, f32[8192]{0:T(1024)}, u32[]{:S(2)}) copy-start(f32[8192]{0:T(1024)} %param.13) | copy-start | bytes 98308
  152.9 14.0 %all-to-all-start = ((bf16[8,16,1024]{2,1,0:T(8,128)(2,1)}), bf16[8,16,1024]{2,1,0:T(8,128)(2,1)S(1)}, u32[]{:S(2)}, u32[]{:S(2)}) async-start(bf16[8,16,1024]{2,1,0:T(8,128)(2,1)} %fusion.9), calls=%async_computation | async-start | bytes 524288 | tf_op jit(solution)/shard_map/all_to_all | solution.py:14
  157.5 69.6 %reduce-scatter.2.cloned.1.call-start = ((), (), s32[]{:S(2)}) async-start(), calls=%async_computation.5 | async-start | bytes 1474560 | tf_op jit(solution)/shard_map/reduce_scatter | solution.py:46
  166.9 1.6 copy-start.1
  166.9 16.0 %slice-start = ((s8[10485760]{0:T(1024)(128)(4,1)}), s8[4194304]{0:T(1024)(128)(4,1)S(1)}, s32[]{:S(2)}) async-start(s8[10485760]{0:T(1024)(128)(4,1)} %bitcast.47), calls=%async_computation.6 | async-start | bytes 8388608
  168.5 14.5 %slice-start.1 = ((s8[10485760]{0:T(1024)(128)(4,1)}), s8[4194304]{0:T(1024)(128)(4,1)S(1)}, s32[]{:S(2)}) async-start(s8[10485760]{0:T(1024)(128)(4,1)} %bitcast.47), calls=%async_computation.7 | async-start | bytes 8388608
  170.0 13.0 %slice-start.2 = ((s8[10485760]{0:T(1024)(128)(4,1)}), s8[2097152]{0:T(1024)(128)(4,1)S(1)}, s32[]{:S(2)}) async-start(s8[10485760]{0:T(1024)(128)(4,1)} %bitcast.47), calls=%async_computation.8 | async-start | bytes 4194304
Sparse Core Ops, SparseCore 0:
  9.6 26.1 all-gather.2
  37.6 104.4 all-gather.4
  187.7 35.0 reduce-scatter.1
